TPU v7x, 128 devices: a whole 4x4x4 slice. The times are simulated.
128 devices in a mesh: rep: 8 (over z, core), tensor: 16 (over y, x).
Axes of the slice: x: 4, y: 4, z: 4, core: 2. Of those that a mesh axis runs over, the one named last changes fastest.
Arguments:
- x_pre: bfloat16 [8192, 2560], P(('rep', 'tensor')), may hold values from -6 to 6
- x_dec: bfloat16 [16, 2560], replicated, may hold values from -6 to 6
- prefix_kv: bfloat16 [8, 4096, 32, 160], P('rep', None, 'tensor'), may hold values from -400 to 400
- cache_kv: bfloat16 [16, 4096, 32, 160], P(None, 'rep', 'tensor'), may hold values from -400 to 400
- dec_len: int32 [16], replicated, may hold values from 1 to 4096, as said below
- offsets: int32 [8], P('rep'), may hold values from 0 to 4096, as said below
- segments: int32 [8, 1024], P('rep'), may hold values from 0 to 3, never falling along the last dimension, each value on 1 to 512 neighbouring positions
- w_qkv: bfloat16 [2560, 7680], P(None, 'tensor'), may hold values from -0.125 to 0.125
- w_out: bfloat16 [2560, 2560], P('tensor'), may hold values from -0.125 to 0.125
- w_up: bfloat16 [2560, 10240], P(None, 'tensor'), may hold values from -0.125 to 0.125
- up_bias: float32 [10240], P('tensor'), may hold values from -3 to 3
- w_down: bfloat16 [10240, 2560], P('tensor'), may hold values from -0.0625 to 0.0625
- biases: float32 [2, 2560], replicated, may hold values from -3 to 3
- gains: float32 [2, 2560], replicated, may hold values from 0.1 to 1.9
- shifts: float32 [2, 2560], replicated, may hold values from -2.5 to 2.5
- w_next: bfloat16 [2560, 7680], P(None, 'tensor'), may hold values from -0.125 to 0.125
Outputs:
- layer_out: bfloat16 [8192, 2560], P(('rep', 'tensor'))
- next_qkv: bfloat16 [8192, 7680], P('rep', 'tensor')
- dec_out: bfloat16 [16, 2560], replicated
- dec_next_qkv: bfloat16 [16, 7680], P(None, 'tensor')
Inputs may be any that keep to these rules, and one draw needn't show every extreme that they name: Request r's cache holds live entries at positions below dec_len[r]; in every draw one request's cache is full (4096) and one request has a single live position. `offsets`: in every draw one span has a full earlier cache (4096 positions) and one span has none.
All inputs are finite; a program needn't handle non-finite values.
Results may differ from a plain program's by a relative error of at most 0.025.
Values may be sent and summed in bfloat16 or wider, within the bound.
A program may use at most 192 MiB of HBM per device.

v0:
```python
import jax
import jax.numpy as jnp
from jax import lax
from jax.sharding import PartitionSpec as P

NEG = -1e30


def combined_all(value, axis, join):
    pieces = jax.tree.map(lambda part: lax.all_gather(part, axis), value)
    head = jax.tree.map(lambda part: part[0], pieces)
    tail = jax.tree.map(lambda part: part[1:], pieces)
    total, _ = lax.scan(lambda total, slab: (join(total, slab), None), head, tail)
    return total


def layer_norm(values, gain_row, shift_row):
    average = jnp.mean(values, axis=-1, keepdims=True)
    centred = values - average
    spread = jnp.mean(centred * centred, axis=-1, keepdims=True)
    return centred * lax.rsqrt(spread + 1e-05) * gain_row + shift_row


def visible(seg_query, query_pos, seg_all, offset, prefix_len):
    prefix_pos = jnp.arange(prefix_len)
    from_prefix = (prefix_pos[None, :] < offset) & (seg_query[:, None] == 0)
    span_pos = jnp.arange(seg_all.shape[0])
    from_span = (seg_all[None, :] == seg_query[:, None]) & (span_pos[None, :] <= query_pos[:, None])
    return jnp.concatenate([from_prefix, from_span], axis=1)


def combine(earlier, later):
    high_early, total_early, output_early = earlier
    high_later, total_later, output_later = later
    highest = jnp.maximum(high_early, high_later)
    factor_early = jnp.exp(high_early - highest)
    factor_later = jnp.exp(high_later - highest)
    return (
        highest,
        total_early * factor_early + total_later * factor_later,
        output_early * factor_early[..., None] + output_later * factor_later[..., None],
    )


def block_state(queries, keys, values, valid, scale):
    scores = jnp.einsum("rhd,rphd->rhp", queries, keys, preferred_element_type=jnp.float32) * scale
    scores = jnp.where(valid[:, None, :], scores, NEG)
    highest = jnp.max(scores, axis=-1)
    weights = jnp.where(valid[:, None, :], jnp.exp(scores - highest[..., None]), 0.0)
    totals = jnp.sum(weights, axis=-1)
    output = jnp.einsum("rhp,rphd->rhd", weights, values.astype(jnp.float32))
    return (highest, totals, output)


def per_device(
    x_pre,
    x_dec,
    prefix_kv,
    cache_kv,
    dec_len,
    offsets,
    segments,
    w_qkv,
    w_out,
    w_up,
    up_bias,
    w_down,
    biases,
    gains,
    shifts,
    w_next,
):
    heads_dev = prefix_kv.shape[2]
    head_dim = prefix_kv.shape[3] // 2
    prefix_len = prefix_kv.shape[1]
    span_len = segments.shape[1]
    scale = head_dim ** (-0.5)

    def up_rows(piece):
        return jax.nn.gelu(
            jnp.dot(piece, w_up, preferred_element_type=jnp.float32) + up_bias, approximate=False
        ).astype(jnp.bfloat16)

    def next_rows(piece):
        return jnp.dot(piece, w_next, preferred_element_type=jnp.float32).astype(jnp.bfloat16)

    qkv_all = jnp.dot(
        lax.all_gather(x_pre, "tensor", axis=0, tiled=True),
        w_qkv,
        preferred_element_type=jnp.float32,
    ).astype(jnp.bfloat16)
    dec_qkv = jnp.dot(x_dec, w_qkv, preferred_element_type=jnp.float32).astype(jnp.bfloat16)
    dec_four = dec_qkv.reshape(dec_qkv.shape[0], heads_dev, 3, head_dim)
    dec_query = dec_four[:, :, 0]
    positions = cache_kv.shape[1]
    cache_base = lax.axis_index("rep") * positions
    valid = (cache_base + jnp.arange(positions))[None, :] < dec_len[:, None]
    state = block_state(dec_query, cache_kv[..., :head_dim], cache_kv[..., head_dim:], valid, scale)
    is_first = lax.axis_index("rep") == 0
    own_score = (
        jnp.sum(dec_query.astype(jnp.float32) * dec_four[:, :, 1].astype(jnp.float32), axis=-1)
        * scale
    )
    own_state = (
        jnp.where(is_first, own_score, NEG),
        jnp.where(is_first, jnp.ones_like(own_score), jnp.zeros_like(own_score)),
        jnp.where(is_first, dec_four[:, :, 2].astype(jnp.float32), 0.0),
    )
    state = combine(state, own_state)
    merged = combined_all(state, "rep", combine)
    dec_attn = (
        (merged[2] / merged[1][..., None])
        .astype(jnp.bfloat16)
        .reshape(dec_qkv.shape[0], heads_dev * head_dim)
    )
    qkv_four = qkv_all.reshape(span_len, heads_dev, 3, head_dim)
    queries = qkv_four[:, :, 0]
    prefix = prefix_kv[0]
    keys = jnp.concatenate([prefix[:, :, :head_dim], qkv_four[:, :, 1]], axis=0)
    values = jnp.concatenate([prefix[:, :, head_dim:], qkv_four[:, :, 2]], axis=0)
    seg_all = segments[0]
    offset = offsets[0]
    query_block = min(512, span_len)

    def attend_block(index):
        begin = index * query_block
        query_rows = lax.dynamic_slice_in_dim(queries, begin, query_block, 0)
        seg_query = lax.dynamic_slice_in_dim(seg_all, begin, query_block, 0)
        mask = visible(seg_query, begin + jnp.arange(query_block), seg_all, offset, prefix_len)
        scores = (
            jnp.einsum("qhd,khd->hqk", query_rows, keys, preferred_element_type=jnp.float32) * scale
        )
        scores = jnp.where(mask[None], scores, NEG)
        highest = jnp.max(scores, axis=-1, keepdims=True)
        weights = jnp.where(mask[None], jnp.exp(scores - highest), 0.0)
        weights = (weights / jnp.sum(weights, axis=-1, keepdims=True)).astype(jnp.bfloat16)
        return jnp.einsum(
            "hqk,khd->qhd", weights, values, preferred_element_type=jnp.float32
        ).astype(jnp.bfloat16)

    blocks = lax.map(attend_block, jnp.arange(span_len // query_block))
    attn = blocks.reshape(span_len, heads_dev * head_dim)
    attn_part = lax.psum_scatter(
        jnp.dot(attn, w_out, preferred_element_type=jnp.float32).astype(jnp.bfloat16),
        "tensor",
        scatter_dimension=0,
        tiled=True,
    ).astype(jnp.float32)
    dec_sum = lax.psum(
        jnp.dot(dec_attn, w_out, preferred_element_type=jnp.float32).astype(jnp.bfloat16), "tensor"
    ).astype(jnp.float32)
    h_first = layer_norm(
        x_pre.astype(jnp.float32) + attn_part + biases[0], gains[0], shifts[0]
    ).astype(jnp.bfloat16)
    hidden = up_rows(lax.all_gather(h_first, "tensor", axis=0, tiled=True))
    dec_first = layer_norm(
        x_dec.astype(jnp.float32) + dec_sum + biases[0], gains[0], shifts[0]
    ).astype(jnp.bfloat16)
    mlp_part = lax.psum_scatter(
        jnp.dot(hidden, w_down, preferred_element_type=jnp.float32).astype(jnp.bfloat16),
        "tensor",
        scatter_dimension=0,
        tiled=True,
    ).astype(jnp.float32)
    layer_out = layer_norm(
        h_first.astype(jnp.float32) + mlp_part + biases[1], gains[1], shifts[1]
    ).astype(jnp.bfloat16)
    dec_hidden = up_rows(dec_first)
    dec_mlp = lax.psum(
        jnp.dot(dec_hidden, w_down, preferred_element_type=jnp.float32).astype(jnp.bfloat16),
        "tensor",
    ).astype(jnp.float32)
    dec_out = layer_norm(
        dec_first.astype(jnp.float32) + dec_mlp + biases[1], gains[1], shifts[1]
    ).astype(jnp.bfloat16)
    next_qkv = next_rows(lax.all_gather(layer_out, "tensor", axis=0, tiled=True))
    dec_next_qkv = next_rows(dec_out)
    return (layer_out, next_qkv, dec_out, dec_next_qkv)


def solution(mesh):
    placed = (
        P(("rep", "tensor"), None),
        P(),
        P("rep", None, "tensor", None),
        P(None, "rep", "tensor", None),
        P(),
        P("rep"),
        P("rep", None),
        P(None, "tensor"),
        P("tensor", None),
        P(None, "tensor"),
        P("tensor"),
        P("tensor", None),
        P(),
        P(),
        P(),
        P(None, "tensor"),
    )
    return jax.shard_map(
        per_device,
        mesh=mesh,
        in_specs=placed,
        out_specs=(P(("rep", "tensor"), None), P("rep", "tensor"), P(), P(None, "tensor")),
        check_vma=False,
    )
```

profile of v0, /device:TPU:1, one launch (start us, length us, event | category | flops | bytes accessed | tf_op | source)
XLA Modules:
  0.0 648.3 jit_solution(16715024463593659003)
XLA Ops:
  8.0 3.7 fusion.182
  11.7 58.0 %all-gather.5.cloned.1.call-done = bf16[1024,2560]{1,0:T(8,128)(2,1)} async-done(((bf16[64,2560]{1,0:T(8,128)(2,1)}), bf16[1024,2560]{1,0:T(8,128)(2,1)}) %all-gather.5.cloned.1.call-update) | async-done | bytes 5242896 | tf_op jit(solution)/shard_map/all_gather | solution.py:88
  69.7 6.1 convolution_convert_fusion.5
  79.2 101.0 %while.24 = (s32[]{:T(128)}, bf16[2,512,2,80]{1,3,2,0:T(8,128)(2,1)}, s32[]{:T(128)}, s32[2]{0:T(128)S(1)}, s32[1024]{0:T(1024)S(1)}, /*index=5*/s32[1,1024]{1,0...) while((s32[]{:T(128)}, ...), condition=%wide.region_3.4_spmd, body=%wide.region_0.3_spmd.sunk | while | flops 1731291136 | bytes 107183400 | solution.py:141
  80.4 11.4 %fusion.215 = f32[2,512,5120]{2,1,0:T(8,128)} fusion(bf16[5120,2,80]{0,2,1:T(8,128)(2,1)} %get-tuple-element.300, bf16[1024,2,80]{0,2,1:T(8,128)(2,1)} %get-tuple-element.299, s32[]{:T(128)S(6)} %select_n.124), kind=kOutput, calls=%fused_computation.16.clone.1 | convolution fusion | flops 838860800 | bytes 22773764 | tf_op jit(solution)/shard_map/while/body/eval_jaxpr/qhd,khd->hqk/dot_general | solution.py:131
  94.7 25.4 %fusion.217 = (f32[2,512]{1,0:T(2,128)S(1)}, f32[2,512,5120]{2,1,0:T(8,128)}) fusion(f32[2,512,5120]{2,1,0:T(8,128)} %fusion.215, pred[512,5120]{1,0:T(8,128)(4,1)S(1)} %pad_add_fusion.2), kind=kOutput, calls=%fused_computation.273.clone.1 | output fusion | flops 36705280 | bytes 44568576 | tf_op jit(solution)/shard_map/while/body/eval_jaxpr/sub | solution.py:135
  120.1 8.8 %fusion.218 = bf16[2,512,2,80]{1,3,2,0:T(8,128)(2,1)S(1)} fusion(bf16[2,512,2,80]{1,3,2,0:T(8,128)(2,1)S(1)} %copy-done.6, s32[]{:T(128)S(6)} %copy.93, bf16[5120,2,80]{0,2,1:T(8,128)(2,1)S(1)} %copy-done.3, f32[2,512,5120]{2,1,0:T(8,128)} %get-tuple-element.254, f32[2,512]{1,0:T(2,128)S(1)} %get-tuple-element.255), kind=kOutput, calls=%fused_computation.15.clone.1 | convolution fusion | flops 849428480 | bytes 22777860 | tf_op jit(solution)/shard_map/while/body/eval_jaxpr/hqk,khd->qhd/dot_general | solution.py:137
  130.9 11.4 %fusion.215 = f32[2,512,5120]{2,1,0:T(8,128)} fusion(bf16[5120,2,80]{0,2,1:T(8,128)(2,1)} %get-tuple-element.300, bf16[1024,2,80]{0,2,1:T(8,128)(2,1)} %get-tuple-element.299, s32[]{:T(128)S(6)} %select_n.124), kind=kOutput, calls=%fused_computation.16.clone.1 | convolution fusion | flops 838860800 | bytes 22773764 | tf_op jit(solution)/shard_map/while/body/eval_jaxpr/qhd,khd->hqk/dot_general | solution.py:131
  145.2 25.4 %fusion.217 = (f32[2,512]{1,0:T(2,128)S(1)}, f32[2,512,5120]{2,1,0:T(8,128)}) fusion(f32[2,512,5120]{2,1,0:T(8,128)} %fusion.215, pred[512,5120]{1,0:T(8,128)(4,1)S(1)} %pad_add_fusion.2), kind=kOutput, calls=%fused_computation.273.clone.1 | output fusion | flops 36705280 | bytes 44568576 | tf_op jit(solution)/shard_map/while/body/eval_jaxpr/sub | solution.py:135
  170.6 8.8 %fusion.218 = bf16[2,512,2,80]{1,3,2,0:T(8,128)(2,1)S(1)} fusion(bf16[2,512,2,80]{1,3,2,0:T(8,128)(2,1)S(1)} %copy-done.6, s32[]{:T(128)S(6)} %copy.93, bf16[5120,2,80]{0,2,1:T(8,128)(2,1)S(1)} %copy-done.3, f32[2,512,5120]{2,1,0:T(8,128)} %get-tuple-element.254, f32[2,512]{1,0:T(2,128)S(1)} %get-tuple-element.255), kind=kOutput, calls=%fused_computation.15.clone.1 | convolution fusion | flops 849428480 | bytes 22777860 | tf_op jit(solution)/shard_map/while/body/eval_jaxpr/hqk,khd->qhd/dot_general | solution.py:137
  181.5 5.0 convolution_convert_fusion.1
  187.4 76.8 %reduce-scatter.3.cloned.1.call-done = bf16[64,2560]{1,0:T(8,128)(2,1)} async-done(((bf16[1024,2560]{1,0:T(8,128)(2,1)}), bf16[64,2560]{1,0:T(8,128)(2,1)}) %reduce-scatter.3.cloned.1.call-update) | async-done | bytes 327696 | tf_op jit(solution)/shard_map/reduce_scatter | solution.py:143
  279.1 14.9 %all-gather = f32[128,2,80]{2,1,0:T(2,128)S(1)} all-gather(f32[16,2,80]{2,1,0:T(2,128)S(1)} %multiply_add_fusion), channel_id=2, replica_groups=mesh['rep'=8,'tensor'=16] {'rep'}, dimensions={0}, use_global_device_ids=true | all-gather | bytes 92160 | tf_op jit(solution)/shard_map/all_gather | solution.py:10
  296.2 10.2 %all_gather.26 = f32[8,16,2]{1,2,0:T(2,128)S(1)} all-gather(f32[1,16,2]{1,2,0:T(2,128)S(1)} %get-tuple-element.148), channel_id=1, replica_groups=mesh['rep'=8,'tensor'=16] {'rep'}, dimensions={0}, use_global_device_ids=true | all-gather | bytes 1152 | tf_op jit(solution)/shard_map/all_gather | solution.py:10
  306.4 8.1 %all_gather.27 = f32[8,16,2]{1,2,0:T(2,128)S(1)} all-gather(f32[1,16,2]{1,2,0:T(2,128)S(1)} %get-tuple-element.147), channel_id=1, replica_groups=mesh['rep'=8,'tensor'=16] {'rep'}, dimensions={0}, use_global_device_ids=true | all-gather | bytes 1152 | tf_op jit(solution)/shard_map/all_gather | solution.py:10
  314.5 7.4 %while.25 = (s32[]{:T(128)}, f32[16,2]{0,1:T(2,128)S(1)}, f32[16,2]{0,1:T(2,128)S(1)}, f32[16,2,80]{2,1,0:T(2,128)S(1)}, f32[7,16,2]{1,2,0:T(2,128)S(1)}, /*inde...) while((s32[]{:T(128)}, f32[16,2]{0,1:T(2,128)S(1)}, f32[16,2]{0,1:T(2,128)S(1)}, ...), condition=%wide.region_14.15_spmd, body=%wide.region_13.14_spmd.sunk | while | flops 7874 | bytes 32613 | solution.py:13
  325.7 17.9 %convolution_convert_fusion = bf16[1024,2560]{1,0:T(8,128)(2,1)} fusion(bf16[640,2560]{1,0:T(8,128)(2,1)S(1)} %copy-done, bf16[1024,2560]{1,0:T(8,128)(2,1)} %all-gather.7.cloned.1.call-done, bf16[2560,640]{1,0:T(8,128)(2,1)} %param.29, f32[640]{0:T(1024)} %param.30), kind=kOutput, calls=%fused_computation.33 | convolution fusion | flops 6756761600 | bytes 17041920 | tf_op jit(solution)/shard_map/dot_general | solution.py:160
  343.8 64.3 %all-reduce.3.cloned.1.call-done = bf16[16,2560]{1,0:T(8,128)(2,1)} async-done(((bf16[16,2560]{1,0:T(8,128)(2,1)}), bf16[16,2560]{1,0:T(8,128)(2,1)}) %all-reduce.3.cloned.1.call-update) | async-done | bytes 81936 | tf_op jit(solution)/shard_map/psum | solution.py:149
  411.2 3.6 convolution_convert_fusion.2
  414.9 75.9 %reduce-scatter.5.cloned.1.call-done = bf16[64,2560]{1,0:T(8,128)(2,1)} async-done(((bf16[1024,2560]{1,0:T(8,128)(2,1)}), bf16[64,2560]{1,0:T(8,128)(2,1)}) %reduce-scatter.5.cloned.1.call-update) | async-done | bytes 327696 | tf_op jit(solution)/shard_map/reduce_scatter | solution.py:159
  495.4 78.8 %all-reduce.5.cloned.1.call-done = bf16[16,2560]{1,0:T(8,128)(2,1)} async-done(((bf16[16,2560]{1,0:T(8,128)(2,1)}), bf16[16,2560]{1,0:T(8,128)(2,1)}) %all-reduce.5.cloned.1.call-update) | async-done | bytes 81936 | tf_op jit(solution)/shard_map/psum | solution.py:169
  577.4 3.1 convolution_convert_fusion.6
  580.5 54.0 %all-gather.9.cloned.1.call-done = bf16[1024,2560]{1,0:T(8,128)(2,1)} async-done(((bf16[64,2560]{1,0:T(8,128)(2,1)}), bf16[1024,2560]{1,0:T(8,128)(2,1)}) %all-gather.9.cloned.1.call-update) | async-done | bytes 5242896 | tf_op jit(solution)/shard_map/all_gather | solution.py:176
  634.5 6.9 %convolution_convert_fusion.4 = bf16[1024,480]{0,1:T(8,128)(2,1)} fusion(bf16[1024,2560]{1,0:T(8,128)(2,1)} %all-gather.9.cloned.1.call-done, bf16[2560,480]{0,1:T(8,128)(2,1)} %param.35), kind=kOutput, calls=%fused_computation.62 | convolution fusion | flops 2517073920 | bytes 8683520 | tf_op jit(solution)/shard_map/dot_general | solution.py:85
  (156 shorter events, 53.7 us)
Async XLA Ops:
  7.2 318.6 %copy-start = (bf16[640,2560]{1,0:T(8,128)(2,1)S(1)}, bf16[640,2560]{1,0:T(8,128)(2,1)}, u32[]{:S(2)}) copy-start(bf16[640,2560]{1,0:T(8,128)(2,1)} %param.31) | copy-start | bytes 9830404
  7.2 62.5 %all-gather.5.cloned.1.call-start = ((), (), s32[]{:S(2)}) async-start(), calls=%async_computation.2 | async-start | bytes 5570560 | tf_op jit(solution)/shard_map/all_gather | solution.py:88
  7.9 256.3 %reduce-scatter.3.cloned.1.call-start = ((), (), s32[]{:S(2)}) async-start(), calls=%async_computation.3 | async-start | bytes 5570560 | tf_op jit(solution)/shard_map/reduce_scatter | solution.py:143
  69.7 6.9 %copy-start.2 = (bf16[4096,2,80]{0,2,1:T(8,128)(2,1)S(1)}, bf16[4096,2,80]{0,2,1:T(8,128)(2,1)}, u32[]{:S(2)}) copy-start(bf16[4096,2,80]{0,2,1:T(8,128)(2,1)} %get-tuple-element.139) | copy-start | bytes 3932164
  75.7 1.4 copy-start.1
  77.2 2.0 copy-start.8
  94.7 25.4 %copy-start.3 = (bf16[5120,2,80]{0,2,1:T(8,128)(2,1)S(1)}, bf16[5120,2,80]{0,2,1:T(8,128)(2,1)}, u32[]{:S(2)}) copy-start(bf16[5120,2,80]{0,2,1:T(8,128)(2,1)} %get-tuple-element.301) | copy-start | bytes 4915204 | tf_op jit(solution)/shard_map/while
  94.7 25.4 %copy-start.6 = (bf16[2,512,2,80]{1,3,2,0:T(8,128)(2,1)S(1)}, bf16[2,512,2,80]{1,3,2,0:T(8,128)(2,1)}, u32[]{:S(2)}) copy-start(bf16[2,512,2,80]{1,3,2,0:T(8,128)(2,1)} %get-tuple-element.281) | copy-start | bytes 983044 | tf_op jit(solution)/shard_map/while
  145.1 25.4 %copy-start.3 = (bf16[5120,2,80]{0,2,1:T(8,128)(2,1)S(1)}, bf16[5120,2,80]{0,2,1:T(8,128)(2,1)}, u32[]{:S(2)}) copy-start(bf16[5120,2,80]{0,2,1:T(8,128)(2,1)} %get-tuple-element.301) | copy-start | bytes 4915204 | tf_op jit(solution)/shard_map/while
  145.2 25.4 %copy-start.6 = (bf16[2,512,2,80]{1,3,2,0:T(8,128)(2,1)S(1)}, bf16[2,512,2,80]{1,3,2,0:T(8,128)(2,1)}, u32[]{:S(2)}) copy-start(bf16[2,512,2,80]{1,3,2,0:T(8,128)(2,1)} %get-tuple-element.281) | copy-start | bytes 983044 | tf_op jit(solution)/shard_map/while
  186.5 0.8 copy-start.14
  186.6 82.6 %copy-start.4 = (bf16[16,2560]{1,0:T(8,128)(2,1)S(1)}, bf16[16,2560]{1,0:T(8,128)(2,1)}, u32[]{:S(2)}) copy-start(bf16[16,2560]{1,0:T(8,128)(2,1)} %param.21) | copy-start | bytes 245764
  186.6 139.2 %all-gather.7.cloned.1.call-start = ((), (), s32[]{:S(2)}) async-start(), calls=%async_computation.4 | async-start | bytes 5570560 | tf_op jit(solution)/shard_map/all_gather | solution.py:155
  264.2 8.4 %copy-start.17 = (s32[16]{0:T(128)S(1)}, s32[16]{0:T(128)}, u32[]{:S(2)}) copy-start(s32[16]{0:T(128)} %param.24) | copy-start | bytes 196
  268.9 139.2 %all-reduce.3.cloned.1.call-start = ((), (), s32[]{:S(2)}) async-start(), calls=%async_computation.7 | async-start | bytes 163840 | tf_op jit(solution)/shard_map/psum | solution.py:149
  272.6 2.4 copy-start.15
  274.9 4.0 copy-start.11
  276.3 2.6 copy-start.9
  276.3 2.7 copy-start.10
  324.2 166.5 %reduce-scatter.5.cloned.1.call-start = ((), (), s32[]{:S(2)}) async-start(), calls=%async_computation.5 | async-start | bytes 5570560 | tf_op jit(solution)/shard_map/reduce_scatter | solution.py:159
  343.7 67.5 %copy-start.16 = (f32[640]{0:T(1024)S(1)}, f32[640]{0:T(1024)}, u32[]{:S(2)}) copy-start(f32[640]{0:T(1024)} %param.30) | copy-start | bytes 7684
  343.7 230.6 %all-reduce.5.cloned.1.call-start = ((), (), s32[]{:S(2)}) async-start(), calls=%async_computation.8 | async-start | bytes 163840 | tf_op jit(solution)/shard_map/psum | solution.py:169
  414.9 219.7 %all-gather.9.cloned.1.call-start = ((), (), s32[]{:S(2)}) async-start(), calls=%async_computation.6 | async-start | bytes 5570560 | tf_op jit(solution)/shard_map/all_gather | solution.py:176
  577.4 64.1 %copy-start.5 = (bf16[16,2560]{1,0:T(8,128)(2,1)}, bf16[16,2560]{1,0:T(8,128)(2,1)S(1)}, u32[]{:S(2)}) copy-start(bf16[16,2560]{1,0:T(8,128)(2,1)S(1)} %add_convert_fusion.2) | copy-start | bytes 245764
  (4 other events, 3.0 us)
Sparse Core Ops, SparseCore 0:
  10.2 59.4 all-gather.4
  186.7 77.4 reduce-scatter.2
  269.0 56.6 all-gather.6
  329.4 78.6 all-reduce.2
  411.7 79.0 reduce-scatter.4
  494.8 79.4 all-reduce.4
  577.0 57.4 all-gather.8
where the time goes:
time: 650 us; the launch traced here: 648 us
  waiting for transfers between devices  410 us (63%)
  matrix products  92.4 us (14%)
  other arithmetic  82.2 us (13%)
  blocking collectives  33.2 us (5%)
  between operations  14.4 us (2%)
  local copies, waits for them, and re-layouts  14.1 us (2%)
    psum x1, waiting for transfers between devices, per_device(): lax.psum(jnp.dot(dec_hidden, w_down, preferred_element_type=jnp.float32)....  78.8 us
    reduce_scatter x1, waiting for transfers between devices, per_device(): lax.psum_scatter(jnp.dot(attn, w_out, preferred_element_type=jnp.float32)...  76.8 us
    reduce_scatter x1, waiting for transfers between devices, per_device(): lax.psum_scatter(jnp.dot(hidden, w_down, preferred_element_type=jnp.float...  75.9 us
    psum x1, waiting for transfers between devices, per_device(): lax.psum(jnp.dot(dec_attn, w_out, preferred_element_type=jnp.float32).ast...  64.3 us
    all_gather x1, waiting for transfers between devices, per_device(): lax.all_gather(x_pre, 'tensor', axis=0, tiled=True)  58 us
    all_gather x1, waiting for transfers between devices, per_device(): lax.all_gather(layer_out, 'tensor', axis=0, tiled=True)  54 us
    sub x2, other arithmetic, attend_block(): weights = jnp.where(mask[None], jnp.exp(scores - highest), 0.0)  50.8 us
    all_gather x3, blocking collectives, combined_all(): pieces = jax.tree.map(lambda part: lax.all_gather(part, axis), value)  33.2 us
  transfers between devices with their start and end apart: 7, of which 7 were waited for; matrix products, arithmetic and copies ran while one was open for 9% of the time, Pallas kernels for 0%

commit v1 on v0

--- a/solution.py
+++ b/solution.py
@@ -4,6 +4,13 @@
 from jax.sharding import PartitionSpec as P
 
 NEG = -1e30
+
+
+def exchange_gather(value, axis, dim):
+    n_dev = lax.axis_size(axis)
+    blocks = jnp.stack([value for _ in range(n_dev)])
+    blocks = lax.all_to_all(blocks, axis, split_axis=0, concat_axis=0)
+    return jnp.concatenate(blocks, axis=dim)
 
 
 def combined_all(value, axis, join):
@@ -173,7 +180,7 @@
     dec_out = layer_norm(
         dec_first.astype(jnp.float32) + dec_mlp + biases[1], gains[1], shifts[1]
     ).astype(jnp.bfloat16)
-    next_qkv = next_rows(lax.all_gather(layer_out, "tensor", axis=0, tiled=True))
+    next_qkv = next_rows(exchange_gather(layer_out, "tensor", 0))
     dec_next_qkv = next_rows(dec_out)
     return (layer_out, next_qkv, dec_out, dec_next_qkv)
 

time: 650 us -> 670 us (1.031)
  waiting for transfers between devices: 410 us -> 421 us
    all_gather x1, waiting for transfers between devices: 1.47 us -> 56.8 us  [per_device(): hidden = up_rows(lax.all_gather(h_first, 'tensor', axis=0, tiled=True))]
    all_gather x1 -> x0, waiting for transfers between devices: 54 us -> none  [per_device(): lax.all_gather(layer_out, 'tensor', axis=0, tiled=True)]
    psum x1, waiting for transfers between devices: 64.3 us -> 116 us  [per_device(): lax.psum(jnp.dot(dec_attn, w_out, preferred_element_type=jnp.float32).ast...]
    reduce_scatter x1, waiting for transfers between devices: 75.9 us -> 32.7 us  [per_device(): lax.psum_scatter(jnp.dot(hidden, w_down, preferred_element_type=jnp.float...]
  transfers between devices with their start and end apart: 7 -> 7, of which waited for: 7 -> 6; matrix products, arithmetic and copies ran while one was open for 9% -> 6% of each run, Pallas kernels for 0% -> 0%
where the time goes in v1:
time: 670 us; the launch traced here: 667 us
  waiting for transfers between devices  421 us (63%)
  matrix products  92.5 us (14%)
  other arithmetic  81.5 us (12%)
  blocking collectives  32.1 us (5%)
  local copies, waits for them, and re-layouts  18.5 us (3%)
  between operations  14.4 us (2%)
    psum x1, waiting for transfers between devices, per_device(): lax.psum(jnp.dot(dec_attn, w_out, preferred_element_type=jnp.float32).ast...  116 us
    psum x1, waiting for transfers between devices, per_device(): lax.psum(jnp.dot(dec_hidden, w_down, preferred_element_type=jnp.float32)....  80.4 us
    reduce_scatter x1, waiting for transfers between devices, per_device(): lax.psum_scatter(jnp.dot(attn, w_out, preferred_element_type=jnp.float32)...  76.8 us
    all_gather x1, waiting for transfers between devices, per_device(): lax.all_gather(x_pre, 'tensor', axis=0, tiled=True)  58 us
    all_gather x1, waiting for transfers between devices, per_device(): hidden = up_rows(lax.all_gather(h_first, 'tensor', axis=0, tiled=True))  56.8 us
    sub x2, other arithmetic, attend_block(): weights = jnp.where(mask[None], jnp.exp(scores - highest), 0.0)  50.8 us
    reduce_scatter x1, waiting for transfers between devices, per_device(): lax.psum_scatter(jnp.dot(hidden, w_down, preferred_element_type=jnp.float...  32.7 us
    all_gather x3, blocking collectives, combined_all(): pieces = jax.tree.map(lambda part: lax.all_gather(part, axis), value)  32.1 us
  transfers between devices with their start and end apart: 7, of which 6 were waited for; matrix products, arithmetic and copies ran while one was open for 6% of the time, Pallas kernels for 0%

profile of v1, /device:TPU:1, one launch (start us, length us, event | category | flops | bytes accessed | tf_op | source)
XLA Modules:
  0.0 667.3 jit_solution(16160523475279774402)
XLA Ops:
  8.0 3.7 fusion.182
  11.7 58.0 %all-gather.4.cloned.1.call-done = bf16[1024,2560]{1,0:T(8,128)(2,1)} async-done(((bf16[64,2560]{1,0:T(8,128)(2,1)}), bf16[1024,2560]{1,0:T(8,128)(2,1)}) %all-gather.4.cloned.1.call-update) | async-done | bytes 5242896 | tf_op jit(solution)/shard_map/all_gather | solution.py:95
  69.7 6.1 convolution_convert_fusion.5
  79.2 101.0 %while.24 = (s32[]{:T(128)}, bf16[2,512,2,80]{1,3,2,0:T(8,128)(2,1)}, s32[]{:T(128)}, s32[2]{0:T(128)S(1)}, s32[1024]{0:T(1024)S(1)}, /*index=5*/s32[1,1024]{1,0...) while((s32[]{:T(128)}, ...), condition=%wide.region_3.4_spmd, body=%wide.region_0.3_spmd.sunk | while | flops 1731291136 | bytes 107183400 | solution.py:148
  80.4 11.4 %fusion.215 = f32[2,512,5120]{2,1,0:T(8,128)} fusion(bf16[5120,2,80]{0,2,1:T(8,128)(2,1)} %get-tuple-element.300, bf16[1024,2,80]{0,2,1:T(8,128)(2,1)} %get-tuple-element.299, s32[]{:T(128)S(6)} %select_n.124), kind=kOutput, calls=%fused_computation.16.clone.1 | convolution fusion | flops 838860800 | bytes 22773764 | tf_op jit(solution)/shard_map/while/body/eval_jaxpr/qhd,khd->hqk/dot_general | solution.py:138
  94.7 25.4 %fusion.217 = (f32[2,512]{1,0:T(2,128)S(1)}, f32[2,512,5120]{2,1,0:T(8,128)}) fusion(f32[2,512,5120]{2,1,0:T(8,128)} %fusion.215, pred[512,5120]{1,0:T(8,128)(4,1)S(1)} %pad_add_fusion.2), kind=kOutput, calls=%fused_computation.273.clone.1 | output fusion | flops 36705280 | bytes 44568576 | tf_op jit(solution)/shard_map/while/body/eval_jaxpr/sub | solution.py:142
  120.1 8.8 %fusion.218 = bf16[2,512,2,80]{1,3,2,0:T(8,128)(2,1)S(1)} fusion(bf16[2,512,2,80]{1,3,2,0:T(8,128)(2,1)S(1)} %copy-done.7, s32[]{:T(128)S(6)} %copy.93, bf16[5120,2,80]{0,2,1:T(8,128)(2,1)S(1)} %copy-done.3, f32[2,512,5120]{2,1,0:T(8,128)} %get-tuple-element.254, f32[2,512]{1,0:T(2,128)S(1)} %get-tuple-element.255), kind=kOutput, calls=%fused_computation.15.clone.1 | convolution fusion | flops 849428480 | bytes 22777860 | tf_op jit(solution)/shard_map/while/body/eval_jaxpr/hqk,khd->qhd/dot_general | solution.py:144
  130.9 11.4 %fusion.215 = f32[2,512,5120]{2,1,0:T(8,128)} fusion(bf16[5120,2,80]{0,2,1:T(8,128)(2,1)} %get-tuple-element.300, bf16[1024,2,80]{0,2,1:T(8,128)(2,1)} %get-tuple-element.299, s32[]{:T(128)S(6)} %select_n.124), kind=kOutput, calls=%fused_computation.16.clone.1 | convolution fusion | flops 838860800 | bytes 22773764 | tf_op jit(solution)/shard_map/while/body/eval_jaxpr/qhd,khd->hqk/dot_general | solution.py:138
  145.2 25.4 %fusion.217 = (f32[2,512]{1,0:T(2,128)S(1)}, f32[2,512,5120]{2,1,0:T(8,128)}) fusion(f32[2,512,5120]{2,1,0:T(8,128)} %fusion.215, pred[512,5120]{1,0:T(8,128)(4,1)S(1)} %pad_add_fusion.2), kind=kOutput, calls=%fused_computation.273.clone.1 | output fusion | flops 36705280 | bytes 44568576 | tf_op jit(solution)/shard_map/while/body/eval_jaxpr/sub | solution.py:142
  170.6 8.8 %fusion.218 = bf16[2,512,2,80]{1,3,2,0:T(8,128)(2,1)S(1)} fusion(bf16[2,512,2,80]{1,3,2,0:T(8,128)(2,1)S(1)} %copy-done.7, s32[]{:T(128)S(6)} %copy.93, bf16[5120,2,80]{0,2,1:T(8,128)(2,1)S(1)} %copy-done.3, f32[2,512,5120]{2,1,0:T(8,128)} %get-tuple-element.254, f32[2,512]{1,0:T(2,128)S(1)} %get-tuple-element.255), kind=kOutput, calls=%fused_computation.15.clone.1 | convolution fusion | flops 849428480 | bytes 22777860 | tf_op jit(solution)/shard_map/while/body/eval_jaxpr/hqk,khd->qhd/dot_general | solution.py:144
  181.5 5.0 convolution_convert_fusion.1
  187.4 76.8 %reduce-scatter.3.cloned.1.call-done = bf16[64,2560]{1,0:T(8,128)(2,1)} async-done(((bf16[1024,2560]{1,0:T(8,128)(2,1)}), bf16[64,2560]{1,0:T(8,128)(2,1)}) %reduce-scatter.3.cloned.1.call-update) | async-done | bytes 327696 | tf_op jit(solution)/shard_map/reduce_scatter | solution.py:150
  268.9 56.8 %all-gather.6.cloned.1.call-done = bf16[1024,2560]{1,0:T(8,128)(2,1)} async-done(((bf16[64,2560]{1,0:T(8,128)(2,1)}), bf16[1024,2560]{1,0:T(8,128)(2,1)}) %all-gather.6.cloned.1.call-update) | async-done | bytes 5242896 | tf_op jit(solution)/shard_map/all_gather | solution.py:162
  325.7 17.9 %convolution_convert_fusion = bf16[1024,2560]{1,0:T(8,128)(2,1)} fusion(bf16[640,2560]{1,0:T(8,128)(2,1)S(1)} %copy-done, bf16[1024,2560]{1,0:T(8,128)(2,1)} %all-gather.6.cloned.1.call-done, bf16[2560,640]{1,0:T(8,128)(2,1)} %param.29, f32[640]{0:T(1024)S(1)} %copy-done.17), kind=kOutput, calls=%fused_computation.33 | convolution fusion | flops 6756761600 | bytes 17041920 | tf_op jit(solution)/shard_map/dot_general | solution.py:167
  354.6 13.7 %all-gather = f32[128,2,80]{2,1,0:T(2,128)S(1)} all-gather(f32[16,2,80]{2,1,0:T(2,128)S(1)} %multiply_add_fusion), channel_id=2, replica_groups=mesh['rep'=8,'tensor'=16] {'rep'}, dimensions={0}, use_global_device_ids=true | all-gather | bytes 92160 | tf_op jit(solution)/shard_map/all_gather | solution.py:17
  370.6 10.2 %all_gather.22 = f32[8,16,2]{1,2,0:T(2,128)S(1)} all-gather(f32[1,16,2]{1,2,0:T(2,128)S(1)} %get-tuple-element.148), channel_id=1, replica_groups=mesh['rep'=8,'tensor'=16] {'rep'}, dimensions={0}, use_global_device_ids=true | all-gather | bytes 1152 | tf_op jit(solution)/shard_map/all_gather | solution.py:17
  380.8 8.1 %all_gather.23 = f32[8,16,2]{1,2,0:T(2,128)S(1)} all-gather(f32[1,16,2]{1,2,0:T(2,128)S(1)} %get-tuple-element.147), channel_id=1, replica_groups=mesh['rep'=8,'tensor'=16] {'rep'}, dimensions={0}, use_global_device_ids=true | all-gather | bytes 1152 | tf_op jit(solution)/shard_map/all_gather | solution.py:17
  388.9 32.7 %reduce-scatter.5.cloned.1.call-done = bf16[64,2560]{1,0:T(8,128)(2,1)} async-done(((bf16[1024,2560]{1,0:T(8,128)(2,1)}), bf16[64,2560]{1,0:T(8,128)(2,1)}) %reduce-scatter.5.cloned.1.call-update) | async-done | bytes 327696 | tf_op jit(solution)/shard_map/reduce_scatter | solution.py:166
  429.1 4.8 all-to-all-start
  434.0 7.4 %while.25 = (s32[]{:T(128)}, f32[16,2]{0,1:T(2,128)S(1)}, f32[16,2]{0,1:T(2,128)S(1)}, f32[16,2,80]{2,1,0:T(2,128)S(1)}, f32[7,16,2]{1,2,0:T(2,128)S(1)}, /*inde...) while((s32[]{:T(128)}, f32[16,2]{0,1:T(2,128)S(1)}, f32[16,2]{0,1:T(2,128)S(1)}, ...), condition=%wide.region_14.15_spmd, body=%wide.region_13.14_spmd.sunk | while | flops 7874 | bytes 32613 | solution.py:20
  444.0 116.1 %all-reduce.3.cloned.1.call-done = bf16[16,2560]{1,0:T(8,128)(2,1)} async-done(((bf16[16,2560]{1,0:T(8,128)(2,1)}), bf16[16,2560]{1,0:T(8,128)(2,1)}) %all-reduce.3.cloned.1.call-update) | async-done | bytes 81936 | tf_op jit(solution)/shard_map/psum | solution.py:156
  563.2 3.6 convolution_convert_fusion.2
  566.8 80.4 %all-reduce.5.cloned.1.call-done = bf16[16,2560]{1,0:T(8,128)(2,1)} async-done(((bf16[16,2560]{1,0:T(8,128)(2,1)}), bf16[16,2560]{1,0:T(8,128)(2,1)}) %all-reduce.5.cloned.1.call-update) | async-done | bytes 81936 | tf_op jit(solution)/shard_map/psum | solution.py:176
  653.5 6.9 %convolution_convert_fusion.4 = bf16[1024,480]{0,1:T(8,128)(2,1)} fusion(bf16[1024,2560]{1,0:T(8,128)(2,1)} %bitcast.14, bf16[2560,480]{0,1:T(8,128)(2,1)} %param.35), kind=kOutput, calls=%fused_computation.62 | convolution fusion | flops 2517073920 | bytes 8683520 | tf_op jit(solution)/shard_map/dot_general | solution.py:92
  (160 shorter events, 59.2 us)
Async XLA Ops:
  7.2 318.6 %copy-start = (bf16[640,2560]{1,0:T(8,128)(2,1)S(1)}, bf16[640,2560]{1,0:T(8,128)(2,1)}, u32[]{:S(2)}) copy-start(bf16[640,2560]{1,0:T(8,128)(2,1)} %param.31) | copy-start | bytes 9830404
  7.2 62.5 %all-gather.4.cloned.1.call-start = ((), (), s32[]{:S(2)}) async-start(), calls=%async_computation.3 | async-start | bytes 5570560 | tf_op jit(solution)/shard_map/all_gather | solution.py:95
  7.9 256.3 %reduce-scatter.3.cloned.1.call-start = ((), (), s32[]{:S(2)}) async-start(), calls=%async_computation.4 | async-start | bytes 5570560 | tf_op jit(solution)/shard_map/reduce_scatter | solution.py:150
  69.7 6.9 %copy-start.2 = (bf16[4096,2,80]{0,2,1:T(8,128)(2,1)S(1)}, bf16[4096,2,80]{0,2,1:T(8,128)(2,1)}, u32[]{:S(2)}) copy-start(bf16[4096,2,80]{0,2,1:T(8,128)(2,1)} %get-tuple-element.139) | copy-start | bytes 3932164
  75.7 1.4 copy-start.1
  77.2 2.0 copy-start.9
  94.7 25.4 %copy-start.3 = (bf16[5120,2,80]{0,2,1:T(8,128)(2,1)S(1)}, bf16[5120,2,80]{0,2,1:T(8,128)(2,1)}, u32[]{:S(2)}) copy-start(bf16[5120,2,80]{0,2,1:T(8,128)(2,1)} %get-tuple-element.301) | copy-start | bytes 4915204 | tf_op jit(solution)/shard_map/while
  94.7 25.4 %copy-start.7 = (bf16[2,512,2,80]{1,3,2,0:T(8,128)(2,1)S(1)}, bf16[2,512,2,80]{1,3,2,0:T(8,128)(2,1)}, u32[]{:S(2)}) copy-start(bf16[2,512,2,80]{1,3,2,0:T(8,128)(2,1)} %get-tuple-element.281) | copy-start | bytes 983044 | tf_op jit(solution)/shard_map/while
  145.1 25.4 %copy-start.3 = (bf16[5120,2,80]{0,2,1:T(8,128)(2,1)S(1)}, bf16[5120,2,80]{0,2,1:T(8,128)(2,1)}, u32[]{:S(2)}) copy-start(bf16[5120,2,80]{0,2,1:T(8,128)(2,1)} %get-tuple-element.301) | copy-start | bytes 4915204 | tf_op jit(solution)/shard_map/while
  145.2 25.4 %copy-start.7 = (bf16[2,512,2,80]{1,3,2,0:T(8,128)(2,1)S(1)}, bf16[2,512,2,80]{1,3,2,0:T(8,128)(2,1)}, u32[]{:S(2)}) copy-start(bf16[2,512,2,80]{1,3,2,0:T(8,128)(2,1)} %get-tuple-element.281) | copy-start | bytes 983044 | tf_op jit(solution)/shard_map/while
  186.6 139.2 %copy-start.17 = (f32[640]{0:T(1024)S(1)}, f32[640]{0:T(1024)}, u32[]{:S(2)}) copy-start(f32[640]{0:T(1024)} %param.30) | copy-start | bytes 7684
  186.6 139.1 %all-gather.6.cloned.1.call-start = ((), (), s32[]{:S(2)}) async-start(), calls=%async_computation.5 | async-start | bytes 5570560 | tf_op jit(solution)/shard_map/all_gather | solution.py:162
  268.9 152.7 %reduce-scatter.5.cloned.1.call-start = ((), (), s32[]{:S(2)}) async-start(), calls=%async_computation.6 | async-start | bytes 5570560 | tf_op jit(solution)/shard_map/reduce_scatter | solution.py:166
  343.6 0.9 copy-start.4
  343.7 4.3 copy-start.19
  347.9 2.4 copy-start.16
  350.3 4.2 copy-start.12
  351.7 2.9 copy-start.10
  351.7 2.9 copy-start.11
  429.1 134.1 %copy-start.18 = (f32[640]{0:T(1024)S(1)}, f32[640]{0:T(1024)}, u32[]{:S(2)}) copy-start(f32[640]{0:T(1024)} %param.30) | copy-start | bytes 7684
  429.1 224.4 %all-to-all-start = ((bf16[16,64,2560]{2,1,0:T(8,128)(2,1)}), bf16[16,64,2560]{2,1,0:T(8,128)(2,1)}, u32[]{:S(2)}, u32[]{:S(2)}) async-start(bf16[16,64,2560]{2,1,0:T(8,128)(2,1)} %stack.2), calls=%async_computation.2 | async-start | bytes 10485760 | tf_op jit(solution)/shard_map/all_to_all | solution.py:12
  433.9 126.2 %all-reduce.3.cloned.1.call-start = ((), (), s32[]{:S(2)}) async-start(), calls=%async_computation.7 | async-start | bytes 163840 | tf_op jit(solution)/shard_map/psum | solution.py:156
  443.7 203.5 %all-reduce.5.cloned.1.call-start = ((), (), s32[]{:S(2)}) async-start(), calls=%async_computation.8 | async-start | bytes 163840 | tf_op jit(solution)/shard_map/psum | solution.py:176
  650.4 10.1 %copy-start.6 = (bf16[16,2560]{1,0:T(8,128)(2,1)}, bf16[16,2560]{1,0:T(8,128)(2,1)S(1)}, u32[]{:S(2)}) copy-start(bf16[16,2560]{1,0:T(8,128)(2,1)S(1)} %add_convert_fusion.2) | copy-start | bytes 245764
  (6 other events, 4.5 us)
Sparse Core Ops, SparseCore 0:
  10.2 59.4 all-gather.3
  186.7 77.4 reduce-scatter.2
  269.0 56.6 all-gather.5
  343.8 77.7 reduce-scatter.4
  443.8 116.2 all-reduce.2
  567.0 80.2 all-reduce.4
